TPU v7x, 32 devices: a whole 2x2x4 slice. The times are simulated.
32 devices in a mesh: ctx: 8 (over y, x, core), ch: 4 (over z).
Axes of the slice: x: 2, y: 2, z: 4, core: 2. Of those that a mesh axis runs over, the one named last changes fastest.
Arguments:
- query_act: bfloat16 [4096, 4096], P('ctx', 'ch'), may hold values from -6 to 6
- key_act: bfloat16 [4096, 4096], P('ctx', 'ch'), may hold values from -6 to 6
- value_act: bfloat16 [4096, 4096], P('ctx', 'ch'), may hold values from -6 to 6
- filters: bfloat16 [4096, 128], P('ch'), may hold values from -0.5 to 0.5
- proj_weight: bfloat16 [8192, 4096], P('ctx', 'ch'), may hold values from -0.09375 to 0.09375
- cotangent: bfloat16 [4096, 8192], P('ctx', 'ch'), may hold values from -6 to 6
Outputs:
- grad_query: bfloat16 [4096, 4096], P('ctx', 'ch')
- grad_key: bfloat16 [4096, 4096], P('ctx', 'ch')
- grad_value: bfloat16 [4096, 4096], P('ctx', 'ch')
- grad_filter: float32 [4096, 128], P('ch')
- grad_proj: float32 [8192, 4096], P('ctx', 'ch')
All inputs are finite; a program needn't handle non-finite values.
Results may differ from a plain program's by a relative error of at most 0.0051.
Values may be sent and summed in bfloat16 or wider, within the bound.
A program may use at most 192 MiB of HBM per device.

v0:
```python
import jax
import jax.numpy as jnp
import numpy as np
from jax import lax
from jax.sharding import PartitionSpec as P

TAPS = 128


def from_behind(x, axis, by):
    length = lax.axis_size(axis)
    pairs = [(i, i + by) for i in range(length) if 0 <= i + by < length]
    return lax.ppermute(x, axis, pairs)


def basis(points):
    freqs = points // 2
    phase = (2 * np.arange(freqs)[:, None] + 1) * np.arange(points)[None, :] % (2 * points)
    angle = np.pi * phase / points
    return np.concatenate([np.cos(angle), np.sin(angle)], 0).astype(np.float32)


def split(a):
    a = jnp.asarray(a, jnp.float32)
    hi = a.astype(jnp.bfloat16)
    return (hi, (a - hi.astype(jnp.float32)).astype(jnp.bfloat16))


def dot32(a, b):
    return jnp.dot(a, b, preferred_element_type=jnp.float32)


def forward(table, x):
    hi, lo = split(table)
    return dot32(hi, x) + dot32(lo, x)


def backward(table, y):
    thi, tlo = split(table)
    yhi, ylo = split(y)
    return dot32(thi, yhi) + dot32(thi, ylo) + dot32(tlo, yhi)


def halves(x):
    n = x.shape[0] // 2
    return (x[:n], x[n:])


def times(x, f):
    (xc, xs), (fc, fs) = (halves(x), halves(f))
    return jnp.concatenate([xc * fc - xs * fs, xc * fs + xs * fc], 0)


def times_conj(x, f):
    (xc, xs), (fc, fs) = (halves(x), halves(f))
    return jnp.concatenate([xc * fc + xs * fs, xs * fc - xc * fs], 0)


def shards(query_act, key_act, value_act, filters, proj_weight, cotangent):
    tokens = query_act.shape[0]
    points = tokens + TAPS
    table = basis(points)
    inverse = (table.T / (points // 2)).astype(np.float32)
    gathered = lax.all_gather(cotangent, "ch", axis=1, tiled=True)
    weight = lax.all_gather(proj_weight, "ctx", axis=0, tiled=True)
    query_f = query_act.astype(jnp.float32)
    key_f = key_act.astype(jnp.float32)
    value_f = value_act.astype(jnp.float32)
    product = (key_f * value_f).astype(jnp.bfloat16)
    before = from_behind(product[tokens - TAPS :], "ctx", 1)
    filt_spec = forward(table[:, :TAPS], filters.T)
    prod_spec = forward(table[:, :TAPS], before) + forward(table[:, TAPS:], product)
    mixed = backward(inverse[TAPS:], times(prod_spec, filt_spec))
    gated = (query_f * mixed).astype(jnp.bfloat16)
    partial_grad = lax.dot_general(
        gathered, gated, (((0,), (0,)), ((), ())), preferred_element_type=jnp.float32
    ).astype(jnp.bfloat16)
    grad_proj = lax.psum_scatter(partial_grad, "ctx", scatter_dimension=0, tiled=True).astype(
        jnp.float32
    )
    grad_mix = dot32(gathered, weight)
    grad_query = (grad_mix * mixed).astype(jnp.bfloat16)
    grad_gate = (grad_mix * query_f).astype(jnp.bfloat16)
    after = from_behind(grad_gate[:TAPS], "ctx", -1)
    own_spec = forward(table[:, :tokens], grad_gate)
    gate_spec = own_spec + forward(table[:, tokens:], after)
    lags = inverse[TAPS - np.arange(TAPS)]
    local_filter = backward(lags, times_conj(prod_spec, own_spec))
    grad_filter = lax.psum(local_filter, "ctx").T
    grad_prod = backward(inverse[:tokens], times_conj(gate_spec, filt_spec))
    grad_key = (grad_prod * value_f).astype(jnp.bfloat16)
    grad_value = (grad_prod * key_f).astype(jnp.bfloat16)
    return (grad_query, grad_key, grad_value, grad_filter, grad_proj)


def solution(mesh):
    return jax.shard_map(
        shards,
        mesh=mesh,
        in_specs=(
            P("ctx", "ch"),
            P("ctx", "ch"),
            P("ctx", "ch"),
            P("ch", None),
            P("ctx", "ch"),
            P("ctx", "ch"),
        ),
        out_specs=(P("ctx", "ch"), P("ctx", "ch"), P("ctx", "ch"), P("ch", None), P("ctx", "ch")),
        check_vma=False,
    )
```

profile of v0, /device:TPU:0, one launch (start us, length us, event | category | flops | bytes accessed | tf_op | source)
XLA Modules:
  0.0 497.0 jit_solution(8108205557831197759)
XLA Ops:
  7.2 0.7 all-gather.3.cloned.1.call-update
  8.0 0.7 all-gather.5.cloned.1.call-update
  8.8 1.3 copy.19
  10.1 1.3 copy.20
  12.4 149.5 %all-gather.3.cloned.1.call-done = bf16[512,8192]{1,0:T(8,128)(2,1)} async-done(((bf16[512,2048]{1,0:T(8,128)(2,1)}), bf16[512,8192]{1,0:T(8,128)(2,1)}) %all-gather.3.cloned.1.call-update) | async-done | bytes 8388624 | tf_op jit(solution)/shard_map/all_gather | solution.py:64
  162.0 90.0 %all-gather.5.cloned.1.call-done = bf16[8192,1024]{1,0:T(8,128)(2,1)} async-done(((bf16[1024,1024]{1,0:T(8,128)(2,1)}), bf16[8192,1024]{1,0:T(8,128)(2,1)}) %all-gather.5.cloned.1.call-update) | async-done | bytes 16777232 | tf_op jit(solution)/shard_map/all_gather | solution.py:65
  251.9 14.9 %fusion.6 = (bf16[512,1024]{1,0:T(8,128)(2,1)S(1)}, f32[512,1024]{1,0:T(8,128)S(1)}) fusion(bf16[512,1024]{1,0:T(8,128)(2,1)} %param.14, bf16[512,8192]{1,0:T(8,128)(2,1)} %all-gather.3.cloned.1.call-done, bf16[8192,1024]{1,0:T(8,128)(2,1)} %all-gather.5.cloned.1.call-done), kind=kOutput, calls=%fused_computation.20 | convolution fusion | flops 8591507456 | bytes 29360128 | tf_op jit(solution)/shard_map/dot_general | solution.py:30
  266.9 1.4 collective-permute-start.1
  268.4 0.9 fusion.40
  269.2 0.9 convolution_add_fusion.1
  271.5 0.6 multiply_add_fusion.1
  272.6 1.0 fusion.8
  273.7 1.0 fusion.21
  275.4 2.7 fusion.3
  278.1 6.7 %collective-permute-start = (bf16[128,1024]{0,1:T(8,128)(2,1)S(1)}, bf16[128,1024]{0,1:T(8,128)(2,1)S(1)}, u32[]{:S(2)}, u32[]{:S(2)}) collective-permute-start(bf16[128,1024]{0,1:T(8,128)(2,1)S(1)} %slice.44), channel_id=1, source_target_pairs={{0,4},{4,8},{8,12},{12,16},{16,20},{20,24},{24,28},{1,5},{5,9},{9,... | collective-permute-start | bytes 786440 | tf_op jit(solution)/shard_map/ppermute | solution.py:13
  284.8 0.9 fusion.38
  285.7 0.9 fusion.37
  287.5 0.7 add_add_fusion.1
  288.2 2.5 multiply_add_fusion
  290.7 1.0 fusion.14
  291.8 1.0 fusion.17
  292.8 2.1 multiply_convert_fusion
  294.9 15.9 %convert_bitcast_fusion = bf16[8192,1024]{0,1:T(8,128)(2,1)} fusion(bf16[512,8192]{1,0:T(8,128)(2,1)} %all-gather.3.cloned.1.call-done, f32[512,1024]{1,0:T(8,128)S(1)} %get-tuple-element.24, bf16[512,1024]{1,0:T(8,128)(2,1)S(1)} %copy-done.25), kind=kOutput, calls=%fused_computation | convolution fusion | flops 8599896064 | bytes 28311552 | tf_op jit(solution)/shard_map/dot_general | solution.py:75
  311.0 1.0 copy-done.2
  313.0 0.5 fusion.11
  313.9 1.4 fusion.12
  315.4 2.4 copy.26
  317.7 1.3 copy.25
  319.0 111.5 %reduce-scatter.2.cloned.1.call-done = bf16[1024,1024]{0,1:T(8,128)(2,1)} async-done(((bf16[8192,1024]{0,1:T(8,128)(2,1)}), bf16[1024,1024]{0,1:T(8,128)(2,1)}) %reduce-scatter.2.cloned.1.call-update) | async-done | bytes 2097168 | tf_op jit(solution)/shard_map/reduce_scatter | solution.py:78
  430.5 4.2 copy.27
  434.6 53.9 %all-reduce.2.cloned.1.call-done = f32[1024,128]{1,0:T(8,128)} async-done(((f32[1024,128]{1,0:T(8,128)}), f32[1024,128]{1,0:T(8,128)}) %all-reduce.2.cloned.1.call-update) | async-done | bytes 524304 | tf_op jit(solution)/shard_map/psum | solution.py:89
  488.6 1.9 copy.33
  (67 shorter events, 6.4 us)
Async XLA Ops:
  7.2 4.2 copy-start
  7.2 1.6 copy-start.10
  7.2 154.8 %all-gather.3.cloned.1.call-start = ((), (), s32[]{:S(2)}) async-start(), calls=%async_computation.1 | async-start | bytes 10485760 | tf_op jit(solution)/shard_map/all_gather | solution.py:64
  7.9 2.2 copy-start.11
  7.9 244.0 %all-gather.5.cloned.1.call-start = ((), (), s32[]{:S(2)}) async-start(), calls=%async_computation.2 | async-start | bytes 18874368 | tf_op jit(solution)/shard_map/all_gather | solution.py:65
  8.7 2.7 copy-start.20
  8.7 421.8 %reduce-scatter.2.cloned.1.call-start = ((), (), s32[]{:S(2)}) async-start(), calls=%async_computation.4 | async-start | bytes 18874368 | tf_op jit(solution)/shard_map/reduce_scatter | solution.py:78
  10.1 1.8 copy-start.13
  12.4 255.9 %copy-start.9 = (bf16[640,512]{1,0:T(8,128)(2,1)S(1)}, bf16[640,512]{1,0:T(8,128)(2,1)}, u32[]{:S(2)}) copy-start(bf16[640,512]{1,0:T(8,128)(2,1)} %constant.33) | copy-start | bytes 1966084
  266.9 2.3 copy-start.18
  266.9 3.6 collective-permute-start.1
  269.2 1.2 copy-start.22
  270.1 0.9 copy-start.24
  271.5 1.1 copy-start.8
  273.7 1.2 copy-start.5
  273.7 1.5 copy-start.6
  273.7 1.7 copy-start.12
  275.4 9.4 %copy-start.17 = (bf16[640,512]{1,0:T(8,128)(2,1)S(1)}, bf16[640,512]{1,0:T(8,128)(2,1)}, u32[]{:S(2)}) copy-start(bf16[640,512]{1,0:T(8,128)(2,1)} %constant.28) | copy-start | bytes 1966084
  278.1 7.6 %copy-start.16 = (bf16[640,512]{1,0:T(8,128)(2,1)S(1)}, bf16[640,512]{1,0:T(8,128)(2,1)}, u32[]{:S(2)}) copy-start(bf16[640,512]{1,0:T(8,128)(2,1)} %constant.25) | copy-start | bytes 1966084
  278.1 8.5 %collective-permute-start = (bf16[128,1024]{0,1:T(8,128)(2,1)S(1)}, bf16[128,1024]{0,1:T(8,128)(2,1)S(1)}, u32[]{:S(2)}, u32[]{:S(2)}) collective-permute-start(bf16[128,1024]{0,1:T(8,128)(2,1)S(1)} %slice.44), channel_id=1, source_target_pairs={{0,4},{4,8},{8,12},{12,16},{16,20},{20,24},{24,28},{1,5},{5,9},{9,... | collective-permute-start | bytes 786440 | tf_op jit(solution)/shard_map/ppermute | solution.py:13
  285.7 0.9 copy-start.14
  286.6 0.9 copy-start.21
  288.2 2.5 copy-start.15
  290.7 1.1 copy-start.7
  292.7 2.1 copy-start.25
  310.7 1.3 copy-start.2
  310.7 1.7 copy-start.3
  310.7 1.7 copy-start.19
  310.8 177.8 %all-reduce.2.cloned.1.call-start = ((), (), s32[]{:S(2)}) async-start(), calls=%async_computation.3 | async-start | bytes 1048576 | tf_op jit(solution)/shard_map/psum | solution.py:89
  313.0 0.9 copy-start.23
  315.3 2.4 copy-start.4
  430.5 60.0 %copy-start.1 = (bf16[1024,128]{1,0:T(8,128)(2,1)S(1)}, bf16[1024,128]{1,0:T(8,128)(2,1)}, u32[]{:S(2)}) copy-start(bf16[1024,128]{1,0:T(8,128)(2,1)} %param.17) | copy-start | bytes 786436
Sparse Core Ops, SparseCore 0:
  9.6 152.3 all-gather.2
  163.9 88.0 all-gather.4
  310.9 119.5 reduce-scatter.1
  434.0 54.5 all-reduce.1
where the time goes:
time: 498 us; the launch traced here: 497 us
  waiting for transfers between devices  407 us (82%)
  matrix products  48.7 us (10%)
  local copies, waits for them, and re-layouts  15.9 us (3%)
  between operations  14.1 us (3%)
  starting transfers between devices  8.5 us (2%)
    all_gather x1, waiting for transfers between devices, shards(): gathered = lax.all_gather(cotangent, 'ch', axis=1, tiled=True)  150 us
    reduce_scatter x1, waiting for transfers between devices, shards(): lax.psum_scatter(partial_grad, 'ctx', scatter_dimension=0, tiled=True)  111 us
    all_gather x1, waiting for transfers between devices, shards(): weight = lax.all_gather(proj_weight, 'ctx', axis=0, tiled=True)  90 us
    psum x1, waiting for transfers between devices, shards(): grad_filter = lax.psum(local_filter, 'ctx').T  53.9 us
    dot_general x20, matrix products, dot32(): return jnp.dot(a, b, preferred_element_type=jnp.float32)  32.9 us
    dot_general x1, matrix products, shards(): lax.dot_general(gathered, gated, (((0,), (0,)), ((), ())), preferred_elem...  15.9 us
    unnamed x58, local copies, waits for them, and re-layouts  15.9 us
  transfers between devices with their start and end apart: 6, of which 5 were waited for; matrix products, arithmetic and copies ran while one was open for 4% of the time, Pallas kernels for 0%

commit v1 on v0

--- a/solution.py
+++ b/solution.py
@@ -3,6 +3,7 @@
 import numpy as np
 from jax import lax
 from jax.sharding import PartitionSpec as P
+from jax.lax import all_gather
 
 TAPS = 128
 
@@ -86,7 +87,7 @@
     gate_spec = own_spec + forward(table[:, tokens:], after)
     lags = inverse[TAPS - np.arange(TAPS)]
     local_filter = backward(lags, times_conj(prod_spec, own_spec))
-    grad_filter = lax.psum(local_filter, "ctx").T
+    grad_filter = jnp.sum(all_gather(local_filter, "ctx"), 0).T
     grad_prod = backward(inverse[:tokens], times_conj(gate_spec, filt_spec))
     grad_key = (grad_prod * value_f).astype(jnp.bfloat16)
     grad_value = (grad_prod * key_f).astype(jnp.bfloat16)

time: 498 us -> 466 us (0.936)
  waiting for transfers between devices: 407 us -> 372 us
    psum x1 -> x0, waiting for transfers between devices: 53.9 us -> none  [shards(): grad_filter = lax.psum(local_filter, 'ctx').T]
    all_gather x0 -> x1, waiting for transfers between devices: none -> 16.2 us  [shards(): grad_filter = jnp.sum(all_gather(local_filter, 'ctx'), 0).T]
    unnamed x58 -> x62, local copies, waits for them, and re-layouts: 15.9 us -> 17 us
  transfers between devices with their start and end apart: 6 -> 6, of which waited for: 5 -> 5; matrix products, arithmetic and copies ran while one was open for 4% -> 7% of each run, Pallas kernels for 0% -> 0%
where the time goes in v1:
time: 466 us
  waiting for transfers between devices  372 us (80%)
  matrix products  49.7 us (11%)
  local copies, waits for them, and re-layouts  17.1 us (4%)
  between operations  14.1 us (3%)
  starting transfers between devices  8.28 us (2%)
  other arithmetic  4.82 us (1%)
    all_gather x1, waiting for transfers between devices, shards(): gathered = lax.all_gather(cotangent, 'ch', axis=1, tiled=True)  150 us
    reduce_scatter x1, waiting for transfers between devices, shards(): lax.psum_scatter(partial_grad, 'ctx', scatter_dimension=0, tiled=True)  114 us
    all_gather x1, waiting for transfers between devices, shards(): weight = lax.all_gather(proj_weight, 'ctx', axis=0, tiled=True)  90 us
    dot_general x20, matrix products, dot32(): return jnp.dot(a, b, preferred_element_type=jnp.float32)  33.8 us
    unnamed x62, local copies, waits for them, and re-layouts  17 us
    all_gather x1, waiting for transfers between devices, shards(): grad_filter = jnp.sum(all_gather(local_filter, 'ctx'), 0).T  16.2 us
    dot_general x1, matrix products, shards(): lax.dot_general(gathered, gated, (((0,), (0,)), ((), ())), preferred_elem...  15.9 us
  transfers between devices with their start and end apart: 6, of which 5 were waited for; matrix products, arithmetic and copies ran while one was open for 7% of the time, Pallas kernels for 0%

profile of v1, /device:TPU:0, one launch (start us, length us, event | category | flops | bytes accessed | tf_op | source)
XLA Modules:
  0.0 465.9 jit_solution(12721726044679813946)
XLA Ops:
  7.2 0.7 all-gather.5.cloned.1.call-update
  8.0 0.7 all-gather.7.cloned.1.call-update
  8.8 1.3 copy.19
  10.1 1.3 copy.20
  12.4 149.5 %all-gather.5.cloned.1.call-done = bf16[512,8192]{1,0:T(8,128)(2,1)} async-done(((bf16[512,2048]{1,0:T(8,128)(2,1)}), bf16[512,8192]{1,0:T(8,128)(2,1)}) %all-gather.5.cloned.1.call-update) | async-done | bytes 8388624 | tf_op jit(solution)/shard_map/all_gather | solution.py:65
  162.0 90.0 %all-gather.7.cloned.1.call-done = bf16[8192,1024]{1,0:T(8,128)(2,1)} async-done(((bf16[1024,1024]{1,0:T(8,128)(2,1)}), bf16[8192,1024]{1,0:T(8,128)(2,1)}) %all-gather.7.cloned.1.call-update) | async-done | bytes 16777232 | tf_op jit(solution)/shard_map/all_gather | solution.py:66
  251.9 15.9 %fusion.6 = (bf16[512,1024]{1,0:T(8,128)(2,1)S(1)}, f32[512,1024]{1,0:T(8,128)}) fusion(bf16[512,1024]{1,0:T(8,128)(2,1)} %param.14, bf16[512,8192]{1,0:T(8,128)(2,1)} %all-gather.5.cloned.1.call-done, bf16[8192,1024]{1,0:T(8,128)(2,1)} %all-gather.7.cloned.1.call-done), kind=kOutput, calls=%fused_computation.21 | convolution fusion | flops 8591507456 | bytes 29360128 | tf_op jit(solution)/shard_map/dot_general | solution.py:31
  267.8 1.4 collective-permute-start.1
  269.3 0.9 fusion.39
  270.2 0.9 convolution_add_fusion.1
  272.5 0.6 multiply_add_fusion.1
  273.6 1.0 fusion.8
  274.7 1.0 fusion.20
  276.4 2.7 fusion.3
  279.1 6.7 %collective-permute-start = (bf16[128,1024]{0,1:T(8,128)(2,1)S(1)}, bf16[128,1024]{0,1:T(8,128)(2,1)S(1)}, u32[]{:S(2)}, u32[]{:S(2)}) collective-permute-start(bf16[128,1024]{0,1:T(8,128)(2,1)S(1)} %slice.44), channel_id=1, source_target_pairs={{0,4},{4,8},{8,12},{12,16},{16,20},{20,24},{24,28},{1,5},{5,9},{9,... | collective-permute-start | bytes 786440 | tf_op jit(solution)/shard_map/ppermute | solution.py:14
  285.9 0.9 fusion.37
  286.8 0.9 fusion.36
  288.6 0.6 add_add_fusion.1
  289.2 2.4 multiply_add_fusion
  293.1 1.4 convolution_add_fusion.2
  295.2 1.0 fusion.13
  296.2 1.0 fusion.16
  297.8 2.0 multiply_convert_fusion
  299.9 15.9 %convert_bitcast_fusion = bf16[8192,1024]{0,1:T(8,128)(2,1)} fusion(bf16[512,8192]{1,0:T(8,128)(2,1)} %all-gather.5.cloned.1.call-done, f32[512,1024]{1,0:T(8,128)S(1)} %get-tuple-element.24, bf16[512,1024]{1,0:T(8,128)(2,1)S(1)} %copy-done.27), kind=kOutput, calls=%fused_computation | convolution fusion | flops 8599896064 | bytes 28311552 | tf_op jit(solution)/shard_map/dot_general | solution.py:76
  315.8 1.2 copy-done.5
  317.0 1.3 copy.26
  318.3 1.3 copy.25
  319.6 16.2 %all-gather.9.cloned.1.call-done = f32[1024,1024]{0,1:T(8,128)} async-done(((f32[128,1024]{0,1:T(8,128)}), f32[1024,1024]{0,1:T(8,128)}) %all-gather.9.cloned.1.call-update) | async-done | bytes 4194320 | tf_op jit(solution)/shard_map/all_gather | solution.py:90
  335.8 3.2 copy.32
  339.0 1.8 bitcast_reduce_fusion
  340.8 114.4 %reduce-scatter.2.cloned.1.call-done = bf16[1024,1024]{0,1:T(8,128)(2,1)} async-done(((bf16[8192,1024]{0,1:T(8,128)(2,1)}), bf16[1024,1024]{0,1:T(8,128)(2,1)}) %reduce-scatter.2.cloned.1.call-update) | async-done | bytes 2097168 | tf_op jit(solution)/shard_map/reduce_scatter | solution.py:79
  455.2 4.1 copy.27
  (72 shorter events, 7.5 us)
Async XLA Ops:
  7.2 4.2 copy-start
  7.2 1.6 copy-start.12
  7.2 154.8 %all-gather.5.cloned.1.call-start = ((), (), s32[]{:S(2)}) async-start(), calls=%async_computation.1 | async-start | bytes 10485760 | tf_op jit(solution)/shard_map/all_gather | solution.py:65
  7.9 2.2 copy-start.13
  7.9 244.0 %all-gather.7.cloned.1.call-start = ((), (), s32[]{:S(2)}) async-start(), calls=%async_computation.2 | async-start | bytes 18874368 | tf_op jit(solution)/shard_map/all_gather | solution.py:66
  8.7 2.7 copy-start.21
  8.7 327.1 %all-gather.9.cloned.1.call-start = ((), (), s32[]{:S(2)}) async-start(), calls=%async_computation.4 | async-start | bytes 4718592 | tf_op jit(solution)/shard_map/all_gather | solution.py:90
  10.1 1.8 copy-start.15
  12.4 256.9 %copy-start.11 = (bf16[640,512]{1,0:T(8,128)(2,1)S(1)}, bf16[640,512]{1,0:T(8,128)(2,1)}, u32[]{:S(2)}) copy-start(bf16[640,512]{1,0:T(8,128)(2,1)} %constant.35) | copy-start | bytes 1966084
  267.8 2.3 copy-start.20
  267.8 3.6 collective-permute-start.1
  270.2 1.2 copy-start.24
  271.0 0.9 copy-start.26
  272.5 1.1 copy-start.9
  274.6 1.2 copy-start.6
  274.6 1.5 copy-start.7
  274.7 1.7 copy-start.14
  276.4 9.5 %copy-start.19 = (bf16[640,512]{1,0:T(8,128)(2,1)S(1)}, bf16[640,512]{1,0:T(8,128)(2,1)}, u32[]{:S(2)}) copy-start(bf16[640,512]{1,0:T(8,128)(2,1)} %constant.30) | copy-start | bytes 1966084
  279.1 7.6 %copy-start.18 = (bf16[640,512]{1,0:T(8,128)(2,1)S(1)}, bf16[640,512]{1,0:T(8,128)(2,1)}, u32[]{:S(2)}) copy-start(bf16[640,512]{1,0:T(8,128)(2,1)} %constant.27) | copy-start | bytes 1966084
  279.1 8.5 %collective-permute-start = (bf16[128,1024]{0,1:T(8,128)(2,1)S(1)}, bf16[128,1024]{0,1:T(8,128)(2,1)S(1)}, u32[]{:S(2)}, u32[]{:S(2)}) collective-permute-start(bf16[128,1024]{0,1:T(8,128)(2,1)S(1)} %slice.44), channel_id=1, source_target_pairs={{0,4},{4,8},{8,12},{12,16},{16,20},{20,24},{24,28},{1,5},{5,9},{9,... | collective-permute-start | bytes 786440 | tf_op jit(solution)/shard_map/ppermute | solution.py:14
  287.6 0.9 copy-start.22
  289.2 2.4 copy-start.23
  293.1 1.5 copy-start.2
  293.1 1.9 copy-start.3
  293.1 2.1 copy-start.17
  294.6 160.7 %reduce-scatter.2.cloned.1.call-start = ((), (), s32[]{:S(2)}) async-start(), calls=%async_computation.3 | async-start | bytes 18874368 | tf_op jit(solution)/shard_map/reduce_scatter | solution.py:79
  295.2 1.1 copy-start.8
  296.2 1.6 copy-start.10
  297.8 2.1 copy-start.27
  315.8 1.2 copy-start.5
  315.8 2.5 copy-start.4
  339.0 120.4 %copy-start.1 = (bf16[1024,128]{1,0:T(8,128)(2,1)S(1)}, bf16[1024,128]{1,0:T(8,128)(2,1)}, u32[]{:S(2)}) copy-start(bf16[1024,128]{1,0:T(8,128)(2,1)} %param.17) | copy-start | bytes 786436
  (2 other events, 1.8 us)
Sparse Core Ops, SparseCore 0:
  9.6 152.3 all-gather.4
  163.9 88.0 all-gather.6
  294.7 41.0 all-gather.8
  339.2 115.9 reduce-scatter.1
